TPU v7x, 256 devices: a whole 4x4x8 slice. The times are simulated.
256 devices in a mesh: row: 16 (over y, x), col: 16 (over z, core).
Axes of the slice: x: 4, y: 4, z: 8, core: 2. Of those that a mesh axis runs over, the one named last changes fastest.
Arguments:
- features: bfloat16 [512, 512, 128], P('col')
- diag_inverse: bfloat16 [512, 128, 128], P('col')
- precision_tiles: float32 [16, 16, 32, 128, 128], P('row', 'col'), may hold values from -3 to 3
- inverse_tiles: float32 [16, 16, 32, 128, 128], P('row', 'col'), may hold values from -0.3125 to 0.3125
- slot_rows: int32 [16, 16, 32], replicated, may hold values from 0 to 511, as said below
- slot_columns: int32 [16, 16, 32], replicated, may hold values from 0 to 1, as said below
- owned_columns: int32 [16, 16, 2], replicated, may hold values from 0 to 511, as said below
- live_counts: int32 [16, 16], replicated, may hold values from 1 to 32, as said below
Outputs:
- direction: float32 [16, 16, 32, 128, 128], P('row', 'col')
Inputs may be any that keep to these rules, and one draw needn't show every extreme that they name: `slot_rows`: slot k of every owner names a block-row held by index k // 2 of col, that is one of feature blocks 32 * (k // 2) to 32 * (k // 2) + 31; no pair of block-row and block-column is named by two slots of the whole grid. `slot_columns`: some owner uses every entry of its list. `owned_columns`: an owner's 2 block-columns are distinct and lie among the feature blocks of its own index of col. The live slots of an owner are slots 0 to live_counts - 1; some owner has all 32 slots live.
All inputs are finite; a program needn't handle non-finite values.
Results may differ from a plain program's by a relative error of at most 0.0003.
Values may be sent and summed in bfloat16 or wider, within the bound.
No kernel may reach another device: no remote copies, remote signals or barrier semaphores. Data moves between devices by JAX's collectives and lax.ppermute only.
A program may use at most 128 MiB of HBM per device.

v0:
```python
import jax
import jax.numpy as jnp
from jax import lax
from jax.sharding import PartitionSpec as P

SWEEPS = 4
step_size = 0.3
penalty = 0.6
highest = lax.Precision.HIGHEST


def soft_update(precision_tile, direction, residual):
    shifted = precision_tile + direction - step_size * residual
    return (
        jnp.sign(shifted) * jnp.maximum(jnp.abs(shifted) - step_size * penalty, 0.0)
        - precision_tile
    )


def body(
    features,
    diag_inverse,
    precision_tiles,
    inverse_tiles,
    slot_rows,
    slot_columns,
    owned_columns,
    live_counts,
):
    col_count = lax.axis_size("col")
    row_index = lax.axis_index("row")
    col_index = lax.axis_index("col")
    block_count = features.shape[0]
    sample_count = features.shape[1]
    block_size = features.shape[2]
    slot_count = precision_tiles.shape[2]
    per_source = slot_count // col_count
    row_table = slot_rows[row_index]
    wanted = jnp.take(row_table.reshape(col_count, col_count, per_source), col_index, axis=1)
    local_rows = (wanted - col_index * block_count).reshape(-1)
    send_tiles = jnp.take(features, local_rows, axis=0).reshape(
        col_count, per_source, sample_count, block_size
    )
    send_diag = jnp.take(diag_inverse, local_rows, axis=0).reshape(
        col_count, per_source, block_size, block_size
    )
    row_tiles, row_diag = (
        lax.all_to_all(send_tiles, "col", split_axis=0, concat_axis=0, tiled=True),
        lax.all_to_all(send_diag, "col", split_axis=0, concat_axis=0, tiled=True),
    )
    row_tiles = row_tiles.reshape(slot_count, sample_count, block_size)
    row_diag = row_diag.reshape(slot_count, block_size, block_size).astype(jnp.float32)
    my_lists = slot_columns[row_index, col_index]
    my_owned = owned_columns[row_index, col_index]
    column_ids = jnp.take(my_owned, my_lists)
    local_cols = column_ids - col_index * block_count
    live_mask = (jnp.arange(slot_count) < live_counts[row_index, col_index]).astype(jnp.float32)
    col_tiles = jnp.take(features, local_cols, axis=0)
    covariance = (
        jnp.einsum("kna,knb->kab", row_tiles, col_tiles, preferred_element_type=jnp.float32)
        / sample_count
    )
    tiles_here = inverse_tiles[0, 0]
    theta_here = precision_tiles[0, 0]
    gradient = covariance - tiles_here
    col_diag = jnp.take(diag_inverse, local_cols, axis=0).astype(jnp.float32)
    direction = jnp.zeros_like(gradient)
    for sweep_index in range(SWEEPS):
        residual = gradient
        if sweep_index > 0:
            left_side = jnp.einsum("kab,kbc->kac", row_diag, direction, precision=highest)
            residual = residual + jnp.einsum("kac,kcd->kad", left_side, col_diag, precision=highest)
            products = (
                jnp.einsum("kba,kbc->kac", direction, tiles_here, precision=highest)
                * live_mask[:, None, None]
            )
            onehot = (local_cols[:, None] == jnp.arange(block_count)[None, :]).astype(jnp.float32)
            dense_sums = jnp.einsum("kf,kab->fab", onehot, products, precision=highest)
            summed = lax.psum(dense_sums, "row")
            residual = residual + jnp.einsum(
                "kab,kbc->kac",
                tiles_here,
                jnp.einsum("kf,fab->kab", onehot, summed, precision=highest),
                precision=highest,
            )
        direction = soft_update(theta_here, direction, residual)
    return (direction * live_mask[:, None, None]).reshape(precision_tiles.shape)


def solution(mesh):
    return jax.shard_map(
        body,
        mesh=mesh,
        in_specs=(
            P("col", None, None),
            P("col", None, None),
            P("row", "col", None, None, None),
            P("row", "col", None, None, None),
            P(),
            P(),
            P(),
            P(),
        ),
        out_specs=P("row", "col", None, None, None),
        check_vma=False,
    )
```

profile of v0, /device:TPU:1, one launch (start us, length us, event | category | flops | bytes accessed | tf_op | source)
XLA Modules:
  0.0 511.0 jit_solution(2454693895170861494)
XLA Ops:
  6.5 0.0 copy-start
  6.5 0.8 constant_dynamic-slice_fusion
  7.4 0.5 fusion.89
  7.9 0.7 constant_dynamic-slice_fusion.2
  8.6 0.1 copy.34
  8.7 0.1 copy.14
  8.8 0.1 sub.61
  8.9 2.0 compare_and_fusion
  10.9 5.2 %gather_fusion = bf16[32,512,128]{2,1,0:T(8,128)(2,1)} fusion(bf16[32,512,128]{2,1,0:T(8,128)(2,1)} %param.12, s32[1024]{0:T(1024)S(1)} %pad_clamp_fusion.1), kind=kCustom, calls=%fused_computation.clone | custom fusion | bytes 8388736 | tf_op jit(solution)/shard_map/jit(_take)/gather | solution.py:41
  16.1 4.6 broadcast_select_fusion
  20.7 6.5 %copy.15 = bf16[16,2,512,128]{2,3,1,0:T(8,128)(2,1)} copy(bf16[16,2,512,128]{3,2,1,0:T(8,128)(2,1)} %bitcast.129) | data formatting | bytes 8388608 | tf_op jit(solution)/shard_map/reshape | solution.py:41
  27.2 10.0 %all-to-all-start = ((bf16[16,2,512,128]{2,3,1,0:T(8,128)(2,1)}), bf16[16,2,512,128]{2,3,1,0:T(8,128)(2,1)}, u32[]{:S(2)}, u32[]{:S(2)}) async-start(bf16[16,2,512,128]{2,3,1,0:T(8,128)(2,1)} %copy.15), calls=%async_computation | async-start | bytes 8388608 | tf_op jit(solution)/shard_map/all_to_all | solution.py:48
  37.1 1.3 dynamic_slice.15
  38.4 0.0 copy-done
  38.4 1.6 gather_fusion.2
  40.1 5.2 %gather_fusion.1 = bf16[32,512,128]{2,1,0:T(8,128)(2,1)} fusion(bf16[32,512,128]{2,1,0:T(8,128)(2,1)} %param.12, s32[1024]{0:T(1024)S(1)} %pad_clamp_fusion), kind=kCustom, calls=%fused_computation.2.clone | custom fusion | bytes 8388736 | tf_op jit(solution)/shard_map/jit(_take)/gather | solution.py:58
  45.3 0.6 compare_convert_fusion
  45.9 0.0 copy-start.2
  45.9 2.5 broadcast_select_fusion.2
  48.5 82.3 %all-to-all-done = bf16[16,2,512,128]{2,3,1,0:T(8,128)(2,1)} async-done(((bf16[16,2,512,128]{2,3,1,0:T(8,128)(2,1)}), bf16[16,2,512,128]{2,3,1,0:T(8,128)(2,1)}, u32[]{:S(2)}, u32[]{:S(2)}) %all-to-all-start) | async-done | bytes 4194336 | tf_op jit(solution)/shard_map/all_to_all | solution.py:48
  130.7 5.5 %all-to-all-start.1 = ((bf16[16,2,128,128]{3,2,1,0:T(8,128)(2,1)}), bf16[16,2,128,128]{3,2,1,0:T(8,128)(2,1)}, u32[]{:S(2)}, u32[]{:S(2)}) async-start(bf16[16,2,128,128]{3,2,1,0:T(8,128)(2,1)} %bitcast.130), calls=%async_computation.1 | async-start | bytes 2097152 | tf_op jit(solution)/shard_map/all_to_all | solution.py:49
  136.3 0.2 all-reduce.4.cloned.1.call-start
  136.5 0.0 copy-done.2
  136.5 0.0 copy-start.3
  136.5 4.9 bitcast_subtract_fusion
  141.4 0.0 copy-done.3
  141.4 0.0 copy-start.7
  141.5 4.5 fusion.39
  146.0 0.0 copy-done.7
  146.0 2.5 fusion.36
  148.5 2.5 copy.20
  151.0 0.0 all-reduce.4.cloned.1.call-update
  151.0 0.3 all-reduce.6.cloned.1.call-start
  151.3 1.7 gather_fusion.3
  153.0 11.3 %all-to-all-done.1 = bf16[16,2,128,128]{3,2,1,0:T(8,128)(2,1)} async-done(((bf16[16,2,128,128]{3,2,1,0:T(8,128)(2,1)}), bf16[16,2,128,128]{3,2,1,0:T(8,128)(2,1)}, u32[]{:S(2)}, u32[]{:S(2)}) %all-to-all-start.1) | async-done | bytes 1048608 | tf_op jit(solution)/shard_map/all_to_all | solution.py:49
  164.3 4.8 fusion.62
  169.1 0.0 copy-done.13
  169.1 2.6 fusion.87
  171.7 79.8 %all-reduce.4.cloned.1.call-done = f32[32,128,128]{2,1,0:T(8,128)} async-done(((f32[32,128,128]{2,1,0:T(8,128)}), f32[32,128,128]{2,1,0:T(8,128)}) %all-reduce.4.cloned.1.call-update) | async-done | bytes 2097168 | tf_op jit(solution)/shard_map/psum | solution.py:79
  251.5 4.1 fusion.34
  255.6 0.0 copy-done.4
  255.6 0.0 copy-done.8
  255.6 6.9 %bitcast_subtract_fusion.3 = f32[32,128,128]{2,1,0:T(8,128)S(1)} fusion(f32[1,1,32,128,128]{4,3,2,1,0:T(8,128)S(1)} %copy-done.4, f32[32,128,128]{2,1,0:T(8,128)S(1)} %copy-done.8, f32[32,128,128]{2,1,0:T(8,128)} %fusion.87, f32[1,1,32,128,128]{4,3,2,1,0:T(8,128)S(1)} %copy-done.2, f32[32,128,128]{2,0,1:T(8,128)S(1)} %fusion.34), kind=kOutput, calls=%fused_computation.34 | convolution fusion | flops 815267840 | bytes 12582912 | tf_op jit(solution)/shard_map/kab,kbc->kac/dot_general | solution.py:80
  262.5 4.3 fusion.42
  266.8 2.5 fusion.31
  269.3 2.6 copy.25
  271.9 0.0 all-reduce.6.cloned.1.call-update
  271.9 0.0 all-reduce.8.cloned.1.call-start
  272.0 3.2 fusion.90
  275.1 2.5 fusion.86
  277.7 94.3 %all-reduce.6.cloned.1.call-done = f32[32,128,128]{2,1,0:T(8,128)} async-done(((f32[32,128,128]{2,1,0:T(8,128)}), f32[32,128,128]{2,1,0:T(8,128)}) %all-reduce.6.cloned.1.call-update) | async-done | bytes 2097168 | tf_op jit(solution)/shard_map/psum | solution.py:79
  371.9 4.1 fusion.29
  376.0 6.9 %bitcast_subtract_fusion.2 = f32[32,128,128]{2,1,0:T(8,128)S(1)} fusion(f32[1,1,32,128,128]{4,3,2,1,0:T(8,128)S(1)} %copy-done.5, f32[32,128,128]{2,1,0:T(8,128)} %copy-done.12, f32[32,128,128]{2,1,0:T(8,128)S(1)} %copy-done.9, f32[32,128,128]{2,1,0:T(8,128)} %fusion.86, f32[1,1,32,128,128]{4,3,2,1,0:T(8,128)S(1)} %copy-done.2, f32[32,128,128]{2,0,1:T(8,128)S(1)} %fusion.29), kind=kOutput, calls=%fused_computation.32 | convolution fusion | flops 811073536 | bytes 14680064 | tf_op jit(solution)/shard_map/kab,kbc->kac/dot_general | solution.py:80
  383.0 0.0 copy-start.11
  383.0 4.0 fusion.45
  387.0 2.5 fusion.26
  389.5 2.6 copy.30
  392.1 0.0 all-reduce.8.cloned.1.call-update
  392.1 3.2 fusion.91
  395.3 2.6 fusion.85
  397.8 94.2 %all-reduce.8.cloned.1.call-done = f32[32,128,128]{2,1,0:T(8,128)} async-done(((f32[32,128,128]{2,1,0:T(8,128)}), f32[32,128,128]{2,1,0:T(8,128)}) %all-reduce.8.cloned.1.call-update) | async-done | bytes 2097168 | tf_op jit(solution)/shard_map/psum | solution.py:79
  492.0 4.3 fusion.24
  496.4 0.0 copy-start.1
  496.4 7.9 %fusion.22 = f32[1,1,32,128,128]{4,3,2,1,0:T(8,128)} fusion(f32[1,1,32,128,128]{4,3,2,1,0:T(8,128)S(1)} %copy-done.6, f32[32,128,128]{2,1,0:T(8,128)} %copy-done.11, f32[32,128,128]{2,1,0:T(8,128)S(1)} %copy-done.10, f32[32,128,128]{2,1,0:T(8,128)} %fusion.85, f32[1,1,32,128,128]{4,3,2,1,0:T(8,128)S(1)} %copy-done.2, f32[32,128,128]{2,0,1:T(8,128)S(1)} %fusion.24, ...), kind=kOutput, calls=%fused_computation.39 | convolution fusion | flops 811597824 | bytes 14680192 | tf_op jit(solution)/shard_map/kab,kbc->kac/dot_general | solution.py:80
  (20 shorter events, 0.1 us)
Async XLA Ops:
  6.5 31.9 %copy-start = (bf16[32,128,128]{2,1,0:T(8,128)(2,1)S(1)}, bf16[32,128,128]{2,1,0:T(8,128)(2,1)}, u32[]{:S(2)}) copy-start(bf16[32,128,128]{2,1,0:T(8,128)(2,1)} %param.13) | copy-start | bytes 3145732
  27.2 103.6 %all-to-all-start = ((bf16[16,2,512,128]{2,3,1,0:T(8,128)(2,1)}), bf16[16,2,512,128]{2,3,1,0:T(8,128)(2,1)}, u32[]{:S(2)}, u32[]{:S(2)}) async-start(bf16[16,2,512,128]{2,3,1,0:T(8,128)(2,1)} %copy.15), calls=%async_computation | async-start | bytes 8388608 | tf_op jit(solution)/shard_map/all_to_all | solution.py:48
  45.9 90.6 %copy-start.2 = (f32[1,1,32,128,128]{4,3,2,1,0:T(8,128)S(1)}, f32[1,1,32,128,128]{4,3,2,1,0:T(8,128)}, u32[]{:S(2)}) copy-start(f32[1,1,32,128,128]{4,3,2,1,0:T(8,128)} %param.15) | copy-start | bytes 6291460
  130.7 33.6 %all-to-all-start.1 = ((bf16[16,2,128,128]{3,2,1,0:T(8,128)(2,1)}), bf16[16,2,128,128]{3,2,1,0:T(8,128)(2,1)}, u32[]{:S(2)}, u32[]{:S(2)}) async-start(bf16[16,2,128,128]{3,2,1,0:T(8,128)(2,1)} %bitcast.130), calls=%async_computation.1 | async-start | bytes 2097152 | tf_op jit(solution)/shard_map/all_to_all | solution.py:49
  136.3 115.2 %all-reduce.4.cloned.1.call-start = ((), (), s32[]{:S(2)}) async-start(), calls=%async_computation.2 | async-start | bytes 4194304 | tf_op jit(solution)/shard_map/psum | solution.py:79
  136.5 4.9 copy-start.3
  141.4 4.5 copy-start.7
  151.0 220.9 %all-reduce.6.cloned.1.call-start = ((), (), s32[]{:S(2)}) async-start(), calls=%async_computation.3 | async-start | bytes 4194304 | tf_op jit(solution)/shard_map/psum | solution.py:79
  164.3 4.8 copy-start.13
  251.5 4.1 copy-start.4
  251.5 4.1 copy-start.8
  262.5 4.3 copy-start.12
  271.9 220.1 %all-reduce.8.cloned.1.call-start = ((), (), s32[]{:S(2)}) async-start(), calls=%async_computation.4 | async-start | bytes 4194304 | tf_op jit(solution)/shard_map/psum | solution.py:79
  371.9 4.1 copy-start.5
  371.9 4.1 copy-start.9
  383.0 4.0 copy-start.11
  492.0 4.3 copy-start.6
  492.0 4.3 copy-start.10
  496.4 7.9 %copy-start.1 = (bf16[32,128,128]{2,1,0:T(8,128)(2,1)S(1)}, bf16[32,128,128]{2,1,0:T(8,128)(2,1)}, u32[]{:S(2)}) copy-start(bf16[32,128,128]{2,1,0:T(8,128)(2,1)} %param.13) | copy-start | bytes 3145732
Sparse Core Ops, SparseCore 0:
  151.2 100.2 all-reduce.3
  272.0 99.8 all-reduce.5
  392.2 99.7 all-reduce.7
where the time goes:
time: 514 us; the launch traced here: 511 us
  waiting for transfers between devices  362 us (70%)
  matrix products  78.1 us (15%)
  local copies, waits for them, and re-layouts  31.6 us (6%)
  starting transfers between devices  16 us (3%)
  between operations  13.6 us (3%)
  other arithmetic  9.75 us (2%)
    psum x3, waiting for transfers between devices, body(): summed = lax.psum(dense_sums, 'row')  268 us
    all_to_all x1, waiting for transfers between devices, body(): lax.all_to_all(send_tiles, 'col', split_axis=0, concat_axis=0, tiled=True)  82.3 us
    dot_general x3, matrix products, body(): jnp.einsum('kab,kbc->kac', tiles_here, jnp.einsum('kf,fab->kab', onehot,...  21.7 us
    dot_general x3, matrix products, body(): jnp.einsum('kba,kbc->kac', direction, tiles_here, precision=highest)  12.8 us
    dot_general x3, matrix products, body(): jnp.einsum('kf,fab->kab', onehot, summed, precision=highest)  12.4 us
    all_to_all x1, waiting for transfers between devices, body(): lax.all_to_all(send_diag, 'col', split_axis=0, concat_axis=0, tiled=True)  11.3 us
    dot_general x3, matrix products, body(): jnp.einsum('kab,kbc->kac', row_diag, direction, precision=highest)  11.1 us
  transfers between devices with their start and end apart: 5, of which 5 were waited for; matrix products, arithmetic and copies ran while one was open for 9% of the time, Pallas kernels for 0%

commit v1 on v0

--- a/solution.py
+++ b/solution.py
@@ -76,7 +76,7 @@
             )
             onehot = (local_cols[:, None] == jnp.arange(block_count)[None, :]).astype(jnp.float32)
             dense_sums = jnp.einsum("kf,kab->fab", onehot, products, precision=highest)
-            summed = lax.psum(dense_sums, "row")
+            summed = jnp.sum(lax.all_gather(dense_sums, "row"), axis=0)
             residual = residual + jnp.einsum(
                 "kab,kbc->kac",
                 tiles_here,

time: 514 us -> 855 us (1.66)
  waiting for transfers between devices: 362 us -> 650 us
  other arithmetic: 9.75 us -> 52.6 us
  starting transfers between devices: 16 us -> 27.2 us
    all_gather x0 -> x3, waiting for transfers between devices: none -> 549 us  [body(): summed = jnp.sum(lax.all_gather(dense_sums, 'row'), axis=0)]
    psum x3 -> x0, waiting for transfers between devices: 268 us -> none  [body(): summed = lax.psum(dense_sums, 'row')]
    reduce_sum x0 -> x3, other arithmetic: none -> 42.9 us  [body(): summed = jnp.sum(lax.all_gather(dense_sums, 'row'), axis=0)]
    all_gather x0 -> x3, starting transfers between devices: none -> 11.7 us  [body(): summed = jnp.sum(lax.all_gather(dense_sums, 'row'), axis=0)]
  transfers between devices with their start and end apart: 5 -> 5, of which waited for: 5 -> 5; matrix products, arithmetic and copies ran while one was open for 9% -> 4% of each run, Pallas kernels for 0% -> 0%
where the time goes in v1:
time: 855 us; the launch traced here: 846 us
  waiting for transfers between devices  650 us (76%)
  matrix products  78.4 us (9%)
  other arithmetic  52.6 us (6%)
  starting transfers between devices  27.2 us (3%)
  local copies, waits for them, and re-layouts  24.1 us (3%)
  between operations  13.6 us (2%)
    all_gather x3, waiting for transfers between devices, body(): summed = jnp.sum(lax.all_gather(dense_sums, 'row'), axis=0)  549 us
    all_to_all x1, waiting for transfers between devices, body(): lax.all_to_all(send_tiles, 'col', split_axis=0, concat_axis=0, tiled=True)  86.2 us
    reduce_sum x3, other arithmetic, body(): summed = jnp.sum(lax.all_gather(dense_sums, 'row'), axis=0)  42.9 us
    dot_general x3, matrix products, body(): jnp.einsum('kab,kbc->kac', tiles_here, jnp.einsum('kf,fab->kab', onehot,...  22.1 us
  transfers between devices with their start and end apart: 5, of which 5 were waited for; matrix products, arithmetic and copies ran while one was open for 4% of the time, Pallas kernels for 0%

profile of v1, /device:TPU:1, one launch (start us, length us, event | category | flops | bytes accessed | tf_op | source)
XLA Modules:
  0.0 845.7 jit_solution(18233417532113147031)
XLA Ops:
  6.5 0.0 copy-start
  6.5 0.8 constant_dynamic-slice_fusion
  7.4 0.5 fusion.86
  7.9 0.7 constant_dynamic-slice_fusion.2
  8.6 0.1 copy.55
  8.7 0.1 copy.26
  8.8 0.1 sub.61
  8.9 2.0 compare_and_fusion
  10.9 5.3 gather_fusion
  16.1 4.6 broadcast_select_fusion
  20.8 6.4 copy.27
  27.2 10.0 %all-to-all-start = ((bf16[16,2,512,128]{2,3,1,0:T(8,128)(2,1)}), bf16[16,2,512,128]{2,3,1,0:T(8,128)(2,1)}, u32[]{:S(2)}, u32[]{:S(2)}) async-start(bf16[16,2,512,128]{2,3,1,0:T(8,128)(2,1)} %copy.27), calls=%async_computation | async-start | bytes 8388608 | tf_op jit(solution)/shard_map/all_to_all | solution.py:48
  37.2 0.0 all-gather.7.cloned.1.call-start
  37.2 1.3 dynamic_slice.15
  38.5 5.4 gather_fusion.1
  43.9 0.6 compare_convert_fusion
  44.5 86.2 %all-to-all-done = bf16[16,2,512,128]{2,3,1,0:T(8,128)(2,1)} async-done(((bf16[16,2,512,128]{2,3,1,0:T(8,128)(2,1)}), bf16[16,2,512,128]{2,3,1,0:T(8,128)(2,1)}, u32[]{:S(2)}, u32[]{:S(2)}) %all-to-all-start) | async-done | bytes 4194336 | tf_op jit(solution)/shard_map/all_to_all | solution.py:48
  130.8 0.0 copy-done.2
  130.8 4.9 bitcast_subtract_fusion
  135.7 0.0 copy-done.3
  135.7 0.0 copy-start.7
  135.7 4.5 fusion.33
  140.2 0.0 copy-done.7
  140.2 3.7 fusion.30
  144.0 0.0 all-gather.7.cloned.1.call-update
  144.0 0.0 copy-done
  144.0 1.7 gather_fusion.2
  145.7 2.4 broadcast_select_fusion.2
  148.1 5.5 all-to-all-start.1
  153.7 11.6 %all-gather.9.cloned.1.call-start = ((), (), s32[]{:S(2)}) async-start(), calls=%async_computation.3 | async-start | bytes 35651584 | tf_op jit(solution)/shard_map/all_gather | solution.py:79
  165.3 1.7 gather_fusion.3
  166.9 14.8 %all-to-all-done.1 = bf16[16,2,128,128]{3,2,1,0:T(8,128)(2,1)} async-done(((bf16[16,2,128,128]{3,2,1,0:T(8,128)(2,1)}), bf16[16,2,128,128]{3,2,1,0:T(8,128)(2,1)}, u32[]{:S(2)}, u32[]{:S(2)}) %all-to-all-start.1) | async-done | bytes 1048608 | tf_op jit(solution)/shard_map/all_to_all | solution.py:49
  181.7 4.9 fusion.56
  186.7 0.0 copy-done.13
  186.7 2.6 fusion.84
  189.3 156.3 %all-gather.7.cloned.1.call-done = f32[512,128,128]{2,0,1:T(8,128)} async-done(((f32[32,128,128]{2,0,1:T(8,128)}), f32[512,128,128]{2,0,1:T(8,128)}) %all-gather.7.cloned.1.call-update) | async-done | bytes 33554448 | tf_op jit(solution)/shard_map/all_gather | solution.py:79
  345.6 14.3 %reduce_sum.27 = f32[32,128,128]{2,0,1:T(8,128)} reduce(f32[16,32,128,128]{3,1,0,2:T(8,128)} %bitcast.138, f32[]{:T(128)} %constant.75.clone.1), dimensions={0}, to_apply=%region_0.3 | reduce | flops 7864320 | bytes 35651588 | tf_op jit(solution)/shard_map/reduce_sum | solution.py:79
  359.9 2.8 fusion.65
  362.8 0.0 copy-done.4
  362.8 0.0 copy-done.8
  362.8 6.9 bitcast_subtract_fusion.3
  369.7 0.0 copy-start.12
  369.7 3.8 fusion.36
  373.5 0.0 copy-done.12
  373.5 4.0 fusion.27
  377.5 0.0 all-gather.9.cloned.1.call-update
  377.5 0.0 all-gather.11.cloned.1.call-start
  377.5 3.2 fusion.87
  380.7 2.6 fusion.83
  383.3 196.2 %all-gather.9.cloned.1.call-done = f32[512,128,128]{2,0,1:T(8,128)} async-done(((f32[32,128,128]{2,0,1:T(8,128)}), f32[512,128,128]{2,0,1:T(8,128)}) %all-gather.9.cloned.1.call-update) | async-done | bytes 33554448 | tf_op jit(solution)/shard_map/all_gather | solution.py:79
  579.5 14.3 %reduce_sum.28 = f32[32,128,128]{2,0,1:T(8,128)} reduce(f32[16,32,128,128]{3,1,0,2:T(8,128)} %bitcast.140, f32[]{:T(128)} %constant.75.clone.1), dimensions={0}, to_apply=%region_1.4 | reduce | flops 7864320 | bytes 35651588 | tf_op jit(solution)/shard_map/reduce_sum | solution.py:79
  593.8 2.9 fusion.63
  596.7 7.2 bitcast_subtract_fusion.2
  603.9 0.0 copy-start.11
  603.9 4.0 fusion.39
  607.9 3.7 fusion.24
  611.6 0.0 all-gather.11.cloned.1.call-update
  611.7 3.2 fusion.88
  614.9 2.6 fusion.82
  617.4 196.2 %all-gather.11.cloned.1.call-done = f32[512,128,128]{2,0,1:T(8,128)} async-done(((f32[32,128,128]{2,0,1:T(8,128)}), f32[512,128,128]{2,0,1:T(8,128)}) %all-gather.11.cloned.1.call-update) | async-done | bytes 33554448 | tf_op jit(solution)/shard_map/all_gather | solution.py:79
  813.7 14.3 %reduce_sum.29 = f32[32,128,128]{2,0,1:T(8,128)} reduce(f32[16,32,128,128]{3,1,0,2:T(8,128)} %bitcast.139, f32[]{:T(128)} %constant.75.clone.1), dimensions={0}, to_apply=%region_2.5 | reduce | flops 7864320 | bytes 35651588 | tf_op jit(solution)/shard_map/reduce_sum | solution.py:79
  828.0 2.9 fusion.61
  830.9 0.0 copy-start.1
  830.9 8.0 fusion.22
  (20 shorter events, 0.1 us)
Async XLA Ops:
  6.5 137.5 %copy-start = (bf16[32,128,128]{2,1,0:T(8,128)(2,1)S(1)}, bf16[32,128,128]{2,1,0:T(8,128)(2,1)}, u32[]{:S(2)}) copy-start(bf16[32,128,128]{2,1,0:T(8,128)(2,1)} %param.13) | copy-start | bytes 3145732
  27.2 103.6 %all-to-all-start = ((bf16[16,2,512,128]{2,3,1,0:T(8,128)(2,1)}), bf16[16,2,512,128]{2,3,1,0:T(8,128)(2,1)}, u32[]{:S(2)}, u32[]{:S(2)}) async-start(bf16[16,2,512,128]{2,3,1,0:T(8,128)(2,1)} %copy.27), calls=%async_computation | async-start | bytes 8388608 | tf_op jit(solution)/shard_map/all_to_all | solution.py:48
  37.2 308.4 %all-gather.7.cloned.1.call-start = ((), (), s32[]{:S(2)}) async-start(), calls=%async_computation.2 | async-start | bytes 35651584 | tf_op jit(solution)/shard_map/all_gather | solution.py:79
  38.5 92.3 %copy-start.2 = (f32[1,1,32,128,128]{4,3,2,1,0:T(8,128)S(1)}, f32[1,1,32,128,128]{4,3,2,1,0:T(8,128)}, u32[]{:S(2)}) copy-start(f32[1,1,32,128,128]{4,3,2,1,0:T(8,128)} %param.15) | copy-start | bytes 6291460
  130.8 4.9 copy-start.3
  135.7 4.5 copy-start.7
  148.1 33.6 %all-to-all-start.1 = ((bf16[16,2,128,128]{3,2,1,0:T(8,128)(2,1)}), bf16[16,2,128,128]{3,2,1,0:T(8,128)(2,1)}, u32[]{:S(2)}, u32[]{:S(2)}) async-start(bf16[16,2,128,128]{3,2,1,0:T(8,128)(2,1)} %bitcast.142), calls=%async_computation.1 | async-start | bytes 2097152 | tf_op jit(solution)/shard_map/all_to_all | solution.py:49
  153.7 425.8 %all-gather.9.cloned.1.call-start = ((), (), s32[]{:S(2)}) async-start(), calls=%async_computation.3 | async-start | bytes 35651584 | tf_op jit(solution)/shard_map/all_gather | solution.py:79
  181.7 5.0 copy-start.13
  359.9 2.9 copy-start.4
  359.9 2.9 copy-start.8
  369.7 3.8 copy-start.12
  377.5 436.2 %all-gather.11.cloned.1.call-start = ((), (), s32[]{:S(2)}) async-start(), calls=%async_computation.4 | async-start | bytes 35651584 | tf_op jit(solution)/shard_map/all_gather | solution.py:79
  593.8 2.9 copy-start.5
  593.8 2.9 copy-start.9
  603.9 4.0 copy-start.11
  828.0 2.9 copy-start.6
  828.0 2.9 copy-start.10
  830.9 8.0 copy-start.1
Sparse Core Ops, SparseCore 0:
  144.1 201.4 all-gather.6
  377.6 201.8 all-gather.8
  611.8 201.8 all-gather.10
